TPU v7x, 32 devices: a whole 2x2x4 slice. The times are simulated.
32 devices in a mesh: dp: 2 (over core), expert: 4 (over z), tensor: 4 (over y, x).
Axes of the slice: x: 2, y: 2, z: 4, core: 2. Of those that a mesh axis runs over, the one named last changes fastest.
Arguments:
- tokens: bfloat16 [24, 197, 768], P(('dp', 'expert'))
- cotangent: bfloat16 [24, 197, 768], P(('dp', 'expert')), may hold values from -6 to 6
- expert_ids: int32 [24, 197, 2], P(('dp', 'expert')), may hold values from 0 to 3, as said below
- slot_rank: int32 [24, 197, 2], P(('dp', 'expert')), may hold values from -1 to 368, as said below
- qkv_weight: bfloat16 [3, 768, 768], P(None, None, 'tensor'), may hold values from -0.3125 to 0.3125
- out_weight: bfloat16 [768, 768], P('tensor'), may hold values from -0.625 to 0.625
- router_weight: bfloat16 [768, 4], replicated, may hold values from -0.15625 to 0.15625
- expert_in: bfloat16 [4, 768, 3072], P('expert', None, 'tensor'), may hold values from -0.21875 to 0.21875
- expert_out: bfloat16 [4, 3072, 768], P('expert', 'tensor'), may hold values from -0.875 to 0.875
- gain_attention: float32 [768], replicated, may hold values from 0.25 to 1.75
- gain_experts: float32 [768], replicated, may hold values from 0.25 to 1.75
Outputs:
- block_out: bfloat16 [24, 197, 768], P(('dp', 'expert'))
- grad_tokens: float32 [24, 197, 768], P(('dp', 'expert'))
- grad_qkv: float32 [3, 768, 768], P(None, None, 'tensor')
- grad_out: float32 [768, 768], P('tensor')
- grad_router: float32 [768, 4], replicated
- grad_expert_in: float32 [4, 768, 3072], P('expert', None, 'tensor')
- grad_expert_out: float32 [4, 3072, 768], P('expert', 'tensor')
- grad_gain_attention: float32 [768], replicated
- grad_gain_experts: float32 [768], replicated
- balance_loss: float32 [], replicated
Inputs may be any that keep to these rules, and one draw needn't show every extreme that they name: `expert_ids`: the two experts of a token differ. Within each aligned block of 591 tokens, the pairs that name one expert are ranked: first choices of all the block's tokens in token order, then second choices in token order. A pair's slot_rank is its rank if that is below 369, else -1. In every block some expert has its slot 368 filled and a pair dropped.
All inputs are finite; a program needn't handle non-finite values.
Results may differ from a plain program's by a relative error of at most 0.017.
The roundings to bfloat16 on the way count: a program that leaves them out, or rounds other values in their place, can miss the bound.
Values may be sent and summed in bfloat16 or wider, within the bound.
No kernel may reach another device: no remote copies, remote signals or barrier semaphores. Data moves between devices by JAX's collectives and lax.ppermute only.
A program may use at most 192 MiB of HBM per device.

v0:
```python
import jax
import jax.numpy as jnp
from jax import lax
from jax.sharding import PartitionSpec as P

HD = 64
epsilon = 1e-06


def normalize(values, gain_row):
    center = values - jnp.mean(values, axis=-1, keepdims=True)
    inverse = lax.rsqrt(jnp.mean(center * center, axis=-1, keepdims=True) + epsilon)
    normed = center * inverse
    return (normed, inverse, normed * gain_row)


def normalize_back(upstream, normed, inverse, gain_row):
    scaled = upstream * gain_row
    result = inverse * (
        scaled
        - jnp.mean(scaled, axis=-1, keepdims=True)
        - normed * jnp.mean(scaled * normed, axis=-1, keepdims=True)
    )
    return (result, jnp.sum(upstream * normed, axis=0))


def exact_gelu(values):
    return jax.nn.gelu(values, approximate=False)


def body(
    tokens,
    cotangent,
    expert_ids,
    slot_rank,
    qkv_weight,
    out_weight,
    router_weight,
    expert_in,
    expert_out,
    gain_attention,
    gain_experts,
):
    images, seq_len, model_width = tokens.shape
    token_rows = images * seq_len
    local_width = qkv_weight.shape[2]
    local_heads = local_width // HD
    slice_width = model_width // lax.axis_size("tensor")
    experts = router_weight.shape[1]
    capacity = 5 * token_rows // (2 * experts)
    owners = lax.axis_size("expert")
    per_owner = experts // owners
    slot_total = experts * capacity
    score_scale = HD ** (-0.5)
    inputs = tokens.reshape(token_rows, model_width).astype(jnp.float32)
    normed_one, inverse_one, mixed_one = normalize(inputs, gain_attention)
    entered = mixed_one.astype(jnp.bfloat16)
    project = jnp.einsum(
        "td,cdf->ctf", entered, qkv_weight, preferred_element_type=jnp.float32
    ).astype(jnp.bfloat16)
    projected_heads = project.reshape(3, images, seq_len, local_heads, HD)
    queries, key_rows, value_rows = (projected_heads[0], projected_heads[1], projected_heads[2])
    scores = (
        jnp.einsum("ishe,ithe->ihst", queries, key_rows, preferred_element_type=jnp.float32)
        * score_scale
    )
    log_total = jax.nn.logsumexp(scores, axis=-1, keepdims=True)
    attn_probs = jnp.exp(scores - log_total).astype(jnp.bfloat16)
    attended = jnp.einsum(
        "ihst,ithe->ishe", attn_probs, value_rows, preferred_element_type=jnp.float32
    )
    attended = attended.astype(jnp.bfloat16).reshape(token_rows, local_width)
    attn_part = jnp.dot(attended, out_weight, preferred_element_type=jnp.float32)
    residual = inputs + lax.psum(attn_part, "tensor")
    normed_two, inverse_two, mixed_two = normalize(residual, gain_experts)
    routed = mixed_two.astype(jnp.bfloat16)
    route_prob = jax.nn.softmax(
        jnp.dot(routed, router_weight, preferred_element_type=jnp.float32), axis=-1
    )
    chosen = expert_ids.reshape(token_rows, 2)
    ranked = slot_rank.reshape(token_rows, 2)
    kept_mask = (ranked >= 0).astype(jnp.float32)
    position = jnp.where(ranked >= 0, chosen * capacity + ranked, slot_total).reshape(-1)
    send_rows = (
        jnp.zeros((slot_total, model_width), jnp.bfloat16)
        .at[position]
        .set(jnp.repeat(routed, 2, axis=0), mode="drop")
        .reshape(experts, capacity, model_width)
    )
    fragment = lax.all_to_all(send_rows, "expert", split_axis=0, concat_axis=0, tiled=True)
    grouped = fragment.reshape(owners, per_owner, fragment.shape[1], model_width)
    before = jnp.einsum("sjcd,jdf->sjcf", grouped, expert_in, preferred_element_type=jnp.float32)
    hidden = exact_gelu(before).astype(jnp.bfloat16)
    expert_part = jnp.einsum(
        "sjcf,jfd->sjcd", hidden, expert_out, preferred_element_type=jnp.float32
    )
    produced = lax.psum_scatter(expert_part, "tensor", scatter_dimension=3, tiled=True).astype(
        jnp.bfloat16
    )
    returned = lax.all_to_all(
        produced.reshape(experts, capacity, slice_width),
        "expert",
        split_axis=0,
        concat_axis=0,
        tiled=True,
    )
    returned = lax.all_gather(returned, "tensor", axis=2, tiled=True).reshape(
        slot_total, model_width
    )
    safe_index = jnp.minimum(position, slot_total - 1)
    picked = returned[safe_index].reshape(token_rows, 2, model_width).astype(jnp.float32)
    gate_values = jnp.take_along_axis(route_prob, chosen, axis=1) * kept_mask
    output = residual + jnp.sum(gate_values[:, :, None] * picked, axis=1)
    block_out = output.astype(jnp.bfloat16).reshape(images, seq_len, model_width)
    upstream = cotangent.reshape(token_rows, model_width).astype(jnp.float32)
    gate_grad = jnp.sum(upstream[:, None, :] * picked, axis=-1) * kept_mask
    member = (chosen[:, :, None] == jnp.arange(experts)[None, None, :]).astype(jnp.float32)
    route_grad = jnp.sum(member * gate_grad[:, :, None], axis=1)
    logit_grad = (
        route_prob * (route_grad - jnp.sum(route_grad * route_prob, axis=-1, keepdims=True))
    ).astype(jnp.bfloat16)
    row_grad = (
        (gate_values[:, :, None] * upstream[:, None, :])
        .astype(jnp.bfloat16)
        .reshape(2 * token_rows, model_width)
    )
    grad_send = (
        jnp.zeros((slot_total, model_width), jnp.bfloat16)
        .at[position]
        .set(row_grad, mode="drop")
        .reshape(experts, capacity, model_width)
    )
    grad_arrived = lax.all_to_all(grad_send, "expert", split_axis=0, concat_axis=0, tiled=True)
    grad_arrived = grad_arrived.reshape(owners, per_owner, capacity, model_width)
    hidden_grad = jnp.einsum(
        "sjcd,jfd->sjcf", grad_arrived, expert_out, preferred_element_type=jnp.float32
    )
    grad_expert_out = jnp.einsum(
        "sjcf,sjcd->jfd", hidden, grad_arrived, preferred_element_type=jnp.float32
    )
    pre_grad = jax.vjp(exact_gelu, before)[1](hidden_grad)[0].astype(jnp.bfloat16)
    grad_expert_in = jnp.einsum(
        "sjcd,sjcf->jdf", grouped, pre_grad, preferred_element_type=jnp.float32
    )
    buffer_part = jnp.einsum(
        "sjcf,jdf->sjcd", pre_grad, expert_in, preferred_element_type=jnp.float32
    )
    buffer_share = lax.psum_scatter(buffer_part, "tensor", scatter_dimension=3, tiled=True).astype(
        jnp.bfloat16
    )
    buffer_back = lax.all_to_all(
        buffer_share.reshape(experts, capacity, slice_width),
        "expert",
        split_axis=0,
        concat_axis=0,
        tiled=True,
    )
    buffer_grad = lax.all_gather(buffer_back, "tensor", axis=2, tiled=True).reshape(
        slot_total, model_width
    )
    routed_grad = jnp.sum(
        buffer_grad[safe_index].reshape(token_rows, 2, model_width).astype(jnp.float32)
        * kept_mask[:, :, None],
        axis=1,
    )
    routed_grad = routed_grad + jnp.dot(
        logit_grad, router_weight.T, preferred_element_type=jnp.float32
    )
    grad_router = jnp.einsum("td,te->de", routed, logit_grad, preferred_element_type=jnp.float32)
    from_norm_two, grad_gain_experts = normalize_back(
        routed_grad, normed_two, inverse_two, gain_experts
    )
    residual_grad = upstream + from_norm_two
    attn_grad = residual_grad.astype(jnp.bfloat16)
    grad_out = jnp.einsum("tf,td->fd", attended, attn_grad, preferred_element_type=jnp.float32)
    heads_grad = jnp.dot(attn_grad, out_weight.T, preferred_element_type=jnp.float32).astype(
        jnp.bfloat16
    )
    heads_grad = heads_grad.reshape(images, seq_len, local_heads, HD)
    again = (
        jnp.einsum("ishe,ithe->ihst", queries, key_rows, preferred_element_type=jnp.float32)
        * score_scale
    )
    probs_full = jnp.exp(again - log_total)
    prob_grad = jnp.einsum(
        "ishe,ithe->ihst", heads_grad, value_rows, preferred_element_type=jnp.float32
    )
    value_grad = jnp.einsum(
        "ihst,ishe->ithe",
        probs_full.astype(jnp.bfloat16),
        heads_grad,
        preferred_element_type=jnp.float32,
    )
    score_grad = (
        probs_full * (prob_grad - jnp.sum(prob_grad * probs_full, axis=-1, keepdims=True))
    ).astype(jnp.bfloat16)
    query_grad = (
        jnp.einsum("ihst,ithe->ishe", score_grad, key_rows, preferred_element_type=jnp.float32)
        * score_scale
    )
    key_grad = (
        jnp.einsum("ihst,ishe->ithe", score_grad, queries, preferred_element_type=jnp.float32)
        * score_scale
    )
    project_grad = (
        jnp.stack([query_grad, key_grad, value_grad])
        .astype(jnp.bfloat16)
        .reshape(3, token_rows, local_width)
    )
    grad_qkv = jnp.einsum("td,ctf->cdf", entered, project_grad, preferred_element_type=jnp.float32)
    entered_part = jnp.einsum(
        "ctf,cdf->td", project_grad, qkv_weight, preferred_element_type=jnp.float32
    )
    entered_grad = lax.psum(entered_part.astype(jnp.bfloat16), "tensor").astype(jnp.float32)
    from_norm_one, grad_gain_attention = normalize_back(
        entered_grad, normed_one, inverse_one, gain_attention
    )
    grad_tokens = (residual_grad + from_norm_one).reshape(images, seq_len, model_width)
    counts = jnp.sum(member, axis=(0, 1))
    prob_sum = jnp.sum(route_prob, axis=0)
    grad_qkv, grad_out, grad_router, grad_gain_attention, grad_gain_experts, counts, prob_sum = (
        lax.psum(
            (
                grad_qkv,
                grad_out,
                grad_router,
                grad_gain_attention,
                grad_gain_experts,
                counts,
                prob_sum,
            ),
            ("dp", "expert"),
        )
    )
    grad_expert_in, grad_expert_out = (
        lax.psum(grad_expert_in.astype(jnp.bfloat16), "dp").astype(jnp.float32),
        lax.psum(grad_expert_out.astype(jnp.bfloat16), "dp").astype(jnp.float32),
    )
    token_total = token_rows * lax.axis_size("dp") * lax.axis_size("expert")
    balance_loss = experts * jnp.sum(counts / (2.0 * token_total) * prob_sum / token_total)
    return (
        block_out,
        grad_tokens,
        grad_qkv,
        grad_out,
        grad_router,
        grad_expert_in,
        grad_expert_out,
        grad_gain_attention,
        grad_gain_experts,
        balance_loss,
    )


def solution(mesh):
    placed = (
        P(("dp", "expert"), None, None),
        P(("dp", "expert"), None, None),
        P(("dp", "expert"), None, None),
        P(("dp", "expert"), None, None),
        P(None, None, "tensor"),
        P("tensor", None),
        P(),
        P("expert", None, "tensor"),
        P("expert", "tensor", None),
        P(),
        P(),
    )
    return jax.shard_map(
        body,
        mesh=mesh,
        in_specs=placed,
        out_specs=(
            P(("dp", "expert"), None, None),
            P(("dp", "expert"), None, None),
            P(None, None, "tensor"),
            P("tensor", None),
            P(),
            P("expert", None, "tensor"),
            P("expert", "tensor", None),
            P(),
            P(),
            P(),
        ),
        check_vma=False,
    )
```

profile of v0, /device:TPU:0, one launch (start us, length us, event | category | flops | bytes accessed | tf_op | source)
XLA Modules:
  0.0 862.4 jit_solution(6967606850585133107)
XLA Ops:
  11.9 2.7 fusion.86
  25.3 2.8 fusion.91
  29.1 66.8 %all-reduce.12.cloned.1.call-done = f32[591,768]{1,0:T(8,128)} async-done(((f32[591,768]{1,0:T(8,128)}), f32[591,768]{1,0:T(8,128)}) %all-reduce.12.cloned.1.call-update) | async-done | bytes 1815568 | tf_op jit(solution)/shard_map/psum | solution.py:74
  101.8 3.9 reshape.430
  105.7 9.6 %scatter_custom_fusion = bf16[1476,768]{1,0:T(8,128)(2,1)S(1)} fusion(s32[1182]{0:T(1024)S(1)} %get-tuple-element.23, bf16[1182,768]{1,0:T(8,128)(2,1)} %reshape.430, bf16[]{:T(256)} %constant.55.clone.1), kind=kCustom, calls=%fused_computation.98 | custom fusion | bytes 2267648 | tf_op jit(solution)/shard_map/scatter | solution.py:87
  117.2 4.6 all-to-all-start
  124.7 3.1 mul.276
  127.8 5.5 mul.277
  137.2 15.1 %gather_fusion.2 = f32[1182]{0:T(1024)S(1)} fusion(f32[591,4]{0,1:T(4,128)S(1)} %fusion.75, s32[1182]{0:T(1024)S(1)} %reshape.420), kind=kCustom, calls=%fused_computation.2 | custom fusion | bytes 18912 | tf_op jit(solution)/shard_map/jit(take_along_axis)/gather | solution.py:112
  152.3 14.2 %scatter_custom_fusion.1 = bf16[1476,768]{1,0:T(8,128)(2,1)S(1)} fusion(s32[1182]{0:T(1024)S(1)} %get-tuple-element.23, f32[1182,768]{1,0:T(8,128)} %mul.277, f32[1182]{0:T(1024)S(1)} %select_select_fusion.1, bf16[]{:T(256)} %constant.55.clone.1), kind=kCustom, calls=%fused_computation.60 | custom fusion | flops 1815552 | bytes 5906434 | tf_op jit(solution)/shard_map/scatter | solution.py:130
  168.5 6.3 all-to-all-done
  174.8 3.6 all-to-all-start.2
  178.9 4.0 fusion.48
  182.9 2.2 copy-done.58
  185.1 12.8 %convolution_bitcast_fusion = f32[4,1,369,768]{3,2,0,1:T(8,128)} fusion(bf16[1,768,768]{2,1,0:T(8,128)(2,1)S(1)} %copy-done, f32[4,369,768]{2,1,0:T(8,128)S(1)} %fusion.48), kind=kOutput, calls=%fused_computation.49 | convolution fusion | flops 1814842368 | bytes 10248192 | tf_op jit(solution)/shard_map/sjcf,jfd->sjcd/dot_general | solution.py:94
  197.9 6.6 copy.113
  204.5 26.2 %all-to-all-done.2 = bf16[4,369,768]{2,1,0:T(8,128)(2,1)S(1)} async-done(((bf16[4,369,768]{2,1,0:T(8,128)(2,1)}), bf16[4,369,768]{2,1,0:T(8,128)(2,1)S(1)}, u32[]{:S(2)}, u32[]{:S(2)}) %all-to-all-start.2) | async-done | bytes 2267168 | tf_op jit(solution)/shard_map/all_to_all | solution.py:133
  230.7 13.6 %fusion.6 = bf16[4,1,369,768]{3,2,0,1:T(8,128)(2,1)S(1)} fusion(f32[4,369,768]{2,1,0:T(8,128)} %copy-done.58, bf16[4,369,768]{2,1,0:T(8,128)(2,1)S(1)} %all-to-all-done.2, bf16[1,768,768]{2,1,0:T(8,128)(2,1)S(1)} %copy-done), kind=kOutput, calls=%fused_computation.14 | convolution fusion | flops 1822777344 | bytes 10248192 | tf_op jit(solution)/shard_map/sjcd,jfd->sjcf/dot_general | solution.py:135
  245.7 4.2 fusion.26
  249.8 6.7 copy.119
  256.5 314.8 %all-reduce.19 = (bf16[4,1,369,768]{2,0,1,3:T(4,128)(2,1)}, bf16[4,1,369,768]{2,0,1,3:T(4,128)(2,1)}) all-reduce(f32[4,1,369,768]{2,0,1,3:T(4,128)} %copy.113, f32[4,1,369,768]{2,0,1,3:T(4,128)} %copy.119), channel_id=2, replica_groups=mesh['dp'=2,'expert'=4,'tensor'=4] {'tensor'}, use_global_device_ids=true, to_apply=%region_10.11.clone | all-reduce | flops 2267136 | bytes 13602816
  572.7 15.9 %all_to_all.20 = bf16[4,369,192]{1,2,0:T(8,128)(2,1)S(1)} all-to-all(bf16[4,369,192]{1,2,0:T(8,128)(2,1)S(1)} %copy.114), channel_id=1, replica_groups=mesh['dp'=2,'expert'=4,'tensor'=4] {'expert'}, dimensions={0} | all-to-all | bytes 1133568 | tf_op jit(solution)/shard_map/all_to_all | solution.py:100
  592.1 3.5 all-to-all-start.3
  600.2 9.8 %all-to-all-done.3 = bf16[4,369,192]{1,2,0:T(8,128)(2,1)S(1)} async-done(((bf16[4,369,192]{1,2,0:T(8,128)(2,1)}), bf16[4,369,192]{1,2,0:T(8,128)(2,1)S(1)}, u32[]{:S(2)}, u32[]{:S(2)}) %all-to-all-start.3) | async-done | bytes 566816 | tf_op jit(solution)/shard_map/all_to_all | solution.py:151
  611.3 5.4 fusion.38
  616.7 13.3 %fusion.41 = bf16[1,768,768]{2,1,0:T(8,128)(2,1)} fusion(bf16[4,369,768]{2,1,0:T(8,128)(2,1)S(1)} %all-to-all-done.2, f32[4,369,768]{2,1,0:T(8,128)} %copy-done.58), kind=kOutput, calls=%fused_computation.77 | convolution fusion | flops 1815432192 | bytes 7981056 | tf_op jit(solution)/shard_map/sjcf,sjcd->jfd/dot_general | solution.py:138
  630.4 5.3 reshape.451
  635.7 2.9 copy.141
  638.5 27.1 %all-gather.5.cloned.1.call-done = bf16[4,369,768]{1,0,2:T(4,128)(2,1)} async-done(((bf16[4,369,192]{1,0,2:T(4,128)(2,1)}), bf16[4,369,768]{1,0,2:T(4,128)(2,1)}) %all-gather.5.cloned.1.call-update) | async-done | bytes 2267152 | tf_op jit(solution)/shard_map/all_gather | solution.py:158
  665.6 5.3 reshape.452
  670.9 4.2 copy.142
  675.2 4.9 gather_fusion
  680.1 7.7 gather_fusion.1
  687.7 5.3 reshape.403
  693.0 5.1 reshape.401
  698.1 11.0 %multiply_reduce_fusion = (f32[591,2]{1,0:T(8,128)S(1)}, f32[591,768]{1,0:T(8,128)}) fusion(f32[591,2,768]{2,1,0:T(2,128)} %reshape.401, f32[591,768]{1,0:T(8,128)S(1)} %copy-done.10, f32[591,2]{1,0:T(8,128)S(1)} %select_select_fusion), kind=kLoop, calls=%fused_computation.33 | loop fusion | flops 3176034 | bytes 7271664 | tf_op jit(solution)/shard_map/reduce_sum | solution.py:116
  709.7 6.6 multiply_reduce_fusion.1
  728.1 2.9 convert_element_type.156
  731.0 3.0 convert_element_type.159
  734.0 2.3 reshape.392
  736.5 2.8 fusion.60
  739.3 3.4 convolution_bitcast_fusion.1
  742.7 35.6 %all-reduce.14.cloned.1.call-done = bf16[591,768]{1,0:T(8,128)(2,1)} async-done(((bf16[591,768]{1,0:T(8,128)(2,1)}), bf16[591,768]{1,0:T(8,128)(2,1)}) %all-reduce.14.cloned.1.call-update) | async-done | bytes 907792 | tf_op jit(solution)/shard_map/psum | solution.py:214
  780.4 3.6 fusion.31
  784.1 2.9 reshape.399
  787.0 30.9 %all-reduce.2 = (f32[768,4]{0,1:T(4,128)}, f32[768]{0:T(1024)}, f32[768]{0:T(1024)}, f32[4]{0:T(128)S(1)}, f32[4]{0:T(128)S(1)}) all-reduce(f32[768,4]{0,1:T(4,128)S(1)} %fusion.92, f32[768]{0:T(1024)S(1)} %get-tuple-element.14, f32[768]{0:T(1024)S(1)} %get-tuple-element.10, ...), channel_id=1, replica_groups=mesh['dp'=2,'expert'=4,'tensor'=4] {'dp','expert'}, use_global_device_ids=true, to_apply=%region_26.27 | all-reduce | flops 4616 | bytes 36928 | tf_op jit(solution)/shard_map/psum | solution.py:222
  819.1 30.1 %all-reduce.16.cloned.1.call-done = (f32[3,768,192]{1,2,0:T(8,128)}, f32[192,768]{1,0:T(8,128)}) async-done(((f32[3,768,192]{1,2,0:T(8,128)}, f32[192,768]{1,0:T(8,128)}), (f32[3,768,192]{1,2,0:T(8,128)}, f32[192,768]{1,0:T(8,128)})) %all-reduce.16.cloned.1.call-update) | async-done | bytes 2359312 | tf_op jit(solution)/shard_map/psum | solution.py:222
  849.2 2.8 copy.179
  (225 shorter events, 61.8 us)
Async XLA Ops:
  7.2 177.9 %copy-start = (bf16[1,768,768]{2,1,0:T(8,128)(2,1)S(1)}, bf16[1,768,768]{2,1,0:T(8,128)(2,1)}, u32[]{:S(2)}) copy-start(bf16[1,768,768]{2,1,0:T(8,128)(2,1)} %param.19) | copy-start | bytes 3538948
  7.2 4.7 copy-start.46
  7.2 88.7 %all-reduce.12.cloned.1.call-start = ((), (), s32[]{:S(2)}) async-start(), calls=%async_computation.4 | async-start | bytes 3637248 | tf_op jit(solution)/shard_map/psum | solution.py:74
  8.8 5.8 copy-start.37
  11.8 84.1 %copy-start.4 = (f32[591,768]{1,0:T(8,128)}, f32[591,768]{1,0:T(8,128)S(1)}, u32[]{:S(2)}) copy-start(f32[591,768]{1,0:T(8,128)S(1)} %reshape.400) | copy-start | bytes 5446660
  18.7 9.3 %copy-start.16 = (bf16[3,197,3,64]{1,0,3,2:T(4,128)(2,1)}, bf16[3,197,3,64]{1,0,3,2:T(4,128)(2,1)S(1)}, u32[]{:S(2)}) copy-start(bf16[3,197,3,64]{1,0,3,2:T(4,128)(2,1)S(1)} %squeeze.9) | copy-start | bytes 680836
  20.5 7.6 copy-start.43
  20.5 7.6 copy-start.53
  28.0 71.6 %copy-start.44 = (f32[768]{0:T(1024)S(1)}, f32[768]{0:T(1024)}, u32[]{:S(2)}) copy-start(f32[768]{0:T(1024)} %param.21) | copy-start | bytes 9220
  117.2 57.6 %all-to-all-start = ((bf16[4,369,768]{2,1,0:T(8,128)(2,1)}), bf16[4,369,768]{2,1,0:T(8,128)(2,1)}, u32[]{:S(2)}, u32[]{:S(2)}) async-start(bf16[4,369,768]{2,1,0:T(8,128)(2,1)} %reshape.386), calls=%async_computation | async-start | bytes 4620288 | tf_op jit(solution)/shard_map/all_to_all | solution.py:90
  124.7 8.6 copy-start.9
  127.8 5.5 copy-start.56
  127.8 6.7 copy-start.51
  174.8 55.9 %all-to-all-start.2 = ((bf16[4,369,768]{2,1,0:T(8,128)(2,1)}), bf16[4,369,768]{2,1,0:T(8,128)(2,1)S(1)}, u32[]{:S(2)}, u32[]{:S(2)}) async-start(bf16[4,369,768]{2,1,0:T(8,128)(2,1)} %reshape.394), calls=%async_computation.2 | async-start | bytes 4620288 | tf_op jit(solution)/shard_map/all_to_all | solution.py:133
  178.4 451.9 %all-gather.3.cloned.1.call-start = ((), (), s32[]{:S(2)}) async-start(), calls=%async_computation.5 | async-start | bytes 2949120 | tf_op jit(solution)/shard_map/all_gather | solution.py:107
  230.7 15.0 %copy-start.54 = (bf16[1,768,768]{2,1,0:T(8,128)(2,1)S(1)}, bf16[1,768,768]{2,1,0:T(8,128)(2,1)}, u32[]{:S(2)}) copy-start(bf16[1,768,768]{2,1,0:T(8,128)(2,1)} %param.18) | copy-start | bytes 3538948
  571.3 24.5 %copy-start.50 = (pred[3,197,2]{1,2,0:T(4,128)(4,1)S(1)}, pred[3,197,2]{1,2,0:T(4,128)(4,1)}, u32[]{:S(2)}) copy-start(pred[3,197,2]{1,2,0:T(4,128)(4,1)} %copy-done.49) | copy-start | bytes 3550
  571.3 24.5 %copy-start.34 = (s32[3,197,2]{1,0,2:T(4,128)S(1)}, s32[3,197,2]{1,0,2:T(4,128)}, u32[]{:S(2)}) copy-start(s32[3,197,2]{1,0,2:T(4,128)} %copy-done.33) | copy-start | bytes 14188
  571.3 26.7 %copy-start.48 = (s32[1182]{0:T(1024)S(1)}, s32[1182]{0:T(1024)}, u32[]{:S(2)}) copy-start(s32[1182]{0:T(1024)} %get-tuple-element.22) | copy-start | bytes 14188
  592.1 17.9 %all-to-all-start.3 = ((bf16[4,369,192]{1,2,0:T(8,128)(2,1)}), bf16[4,369,192]{1,2,0:T(8,128)(2,1)S(1)}, u32[]{:S(2)}, u32[]{:S(2)}) async-start(bf16[4,369,192]{1,2,0:T(8,128)(2,1)} %copy.120), calls=%async_computation.3 | async-start | bytes 1179648 | tf_op jit(solution)/shard_map/all_to_all | solution.py:151
  595.6 70.1 %all-gather.5.cloned.1.call-start = ((), (), s32[]{:S(2)}) async-start(), calls=%async_computation.6 | async-start | bytes 2949120 | tf_op jit(solution)/shard_map/all_gather | solution.py:158
  611.2 116.9 %all-reduce.18.cloned.1.call-start = ((), (), s32[]{:S(2)}) async-start(), calls=%async_computation.9 | async-start | bytes 4718592 | tf_op jit(solution)/shard_map/psum | solution.py:236
  630.1 148.2 %all-reduce.14.cloned.1.call-start = ((), (), s32[]{:S(2)}) async-start(), calls=%async_computation.7 | async-start | bytes 1818624 | tf_op jit(solution)/shard_map/psum | solution.py:214
  687.7 10.4 %copy-start.10 = (f32[591,768]{1,0:T(8,128)S(1)}, f32[591,768]{1,0:T(8,128)}, u32[]{:S(2)}) copy-start(f32[591,768]{1,0:T(8,128)} %copy-done.9) | copy-start | bytes 5446660
  698.1 11.4 %copy-start.28 = (f32[591,4]{0,1:T(4,128)S(1)}, f32[591,4]{0,1:T(4,128)}, u32[]{:S(2)}) copy-start(f32[591,4]{0,1:T(4,128)} %copy-done.27) | copy-start | bytes 28372
  698.1 11.4 %copy-start.30 = (f32[591]{0:T(1024)S(1)}, f32[591]{0:T(1024)}, u32[]{:S(2)}) copy-start(f32[591]{0:T(1024)} %copy-done.29) | copy-start | bytes 7096
  698.1 11.4 %copy-start.36 = (f32[591]{0:T(1024)S(1)}, f32[591]{0:T(1024)}, u32[]{:S(2)}) copy-start(f32[591]{0:T(1024)} %copy-done.35) | copy-start | bytes 7096
  698.1 11.5 %copy-start.22 = (f32[591,2]{1,0:T(8,128)S(1)}, f32[591,2]{1,0:T(8,128)}, u32[]{:S(2)}) copy-start(f32[591,2]{1,0:T(8,128)} %copy.123) | copy-start | bytes 14188
  709.2 7.2 copy-start.7
  709.2 7.2 copy-start.32
  709.2 7.2 copy-start.42
  709.2 7.2 copy-start.45
  709.2 7.2 copy-start.52
  709.7 7.8 copy-start.8
  709.7 7.8 copy-start.11
  709.7 7.8 copy-start.15
  717.5 2.9 copy-start.23
  717.5 3.6 copy-start.3
  717.5 3.6 copy-start.26
  719.1 3.7 copy-start.17
  727.7 8.6 copy-start.14
  727.7 121.4 %all-reduce.16.cloned.1.call-start = ((), (), s32[]{:S(2)}) async-start(), calls=%async_computation.8 | async-start | bytes 4718592 | tf_op jit(solution)/shard_map/psum | solution.py:222
  728.1 8.4 copy-start.20
  731.0 8.3 copy-start.5
  731.0 8.3 copy-start.38
  731.0 8.3 copy-start.40
  731.0 8.3 copy-start.47
  780.4 73.5 %copy-start.1 = (bf16[1,768,768]{2,1,0:T(8,128)(2,1)S(1)}, bf16[1,768,768]{2,1,0:T(8,128)(2,1)}, u32[]{:S(2)}) copy-start(bf16[1,768,768]{2,1,0:T(8,128)(2,1)} %param.19) | copy-start | bytes 3538948
  (20 other events, 25.4 us)
Sparse Core Ops, SparseCore 0:
  28.2 67.7 all-reduce.11
  590.0 35.5 all-gather.2
  628.1 37.4 all-gather.4
  668.6 21.6 all-reduce.17
  727.9 50.4 all-reduce.13
  781.3 67.7 all-reduce.15
where the time goes:
time: 872 us; the launch traced here: 862 us
  blocking collectives  362 us (42%)
  waiting for transfers between devices  202 us (23%)
  local copies, waits for them, and re-layouts  139 us (16%)
  matrix products  74 us (8%)
  other arithmetic  54.2 us (6%)
  between operations  18 us (2%)
  starting transfers between devices  13 us (1%)
    unnamed x1, blocking collectives  315 us
    psum x1, waiting for transfers between devices, body(): residual = inputs + lax.psum(attn_part, 'tensor')  66.8 us
    psum x1, waiting for transfers between devices, body(): lax.psum(entered_part.astype(jnp.bfloat16), 'tensor').astype(jnp.float32)  35.6 us
    psum x1, blocking collectives, body(): lax.psum((grad_qkv, grad_out, grad_router, grad_gain_attention, grad_gain...  30.9 us
    psum x1, waiting for transfers between devices, body(): lax.psum((grad_qkv, grad_out, grad_router, grad_gain_attention, grad_gain...  30.1 us
    all_gather x1, waiting for transfers between devices, body(): lax.all_gather(buffer_back, 'tensor', axis=2, tiled=True)  27.1 us
    all_to_all x1, waiting for transfers between devices, body(): lax.all_to_all(grad_send, 'expert', split_axis=0, concat_axis=0, tiled=True)  26.2 us
  transfers between devices with their start and end apart: 9, of which 7 were waited for; matrix products, arithmetic and copies ran while one was open for 22% of the time, Pallas kernels for 0%

commit v1 on v0

--- a/solution.py
+++ b/solution.py
@@ -220,16 +220,19 @@
     prob_sum = jnp.sum(route_prob, axis=0)
     grad_qkv, grad_out, grad_router, grad_gain_attention, grad_gain_experts, counts, prob_sum = (
         lax.psum(
-            (
-                grad_qkv,
-                grad_out,
-                grad_router,
-                grad_gain_attention,
-                grad_gain_experts,
-                counts,
-                prob_sum,
+            lax.psum(
+                (
+                    grad_qkv,
+                    grad_out,
+                    grad_router,
+                    grad_gain_attention,
+                    grad_gain_experts,
+                    counts,
+                    prob_sum,
+                ),
+                "expert",
             ),
-            ("dp", "expert"),
+            "dp",
         )
     )
     grad_expert_in, grad_expert_out = (

time: 872 us -> 962 us (1.10)
  waiting for transfers between devices: 202 us -> 290 us
    psum x1, waiting for transfers between devices: 30.1 us -> 78.7 us  [body(): lax.psum((grad_qkv, grad_out, grad_router, grad_gain_attention, grad_gain...]
    psum x1, waiting for transfers between devices: 0.02 us -> 23.6 us  [body(): lax.psum(grad_expert_in.astype(jnp.bfloat16), 'dp').astype(jnp.float32)]
    all_to_all x0 -> x1, blocking collectives: none -> 17 us  [body(): lax.all_to_all(buffer_share.reshape(experts, capacity, slice_width), 'exp...]
    psum x1, blocking collectives: 30.9 us -> 19 us  [body(): lax.psum((grad_qkv, grad_out, grad_router, grad_gain_attention, grad_gain...]
    psum x1, waiting for transfers between devices: 35.6 us -> 46.5 us  [body(): lax.psum(entered_part.astype(jnp.bfloat16), 'tensor').astype(jnp.float32)]
    all_to_all x1 -> x0, waiting for transfers between devices: 9.79 us -> none  [body(): lax.all_to_all(buffer_share.reshape(experts, capacity, slice_width), 'exp...]
  transfers between devices with their start and end apart: 9 -> 9, of which waited for: 7 -> 8; matrix products, arithmetic and copies ran while one was open for 22% -> 13% of each run, Pallas kernels for 0% -> 0%
where the time goes in v1:
time: 962 us; the launch traced here: 953 us
  blocking collectives  371 us (39%)
  waiting for transfers between devices  290 us (30%)
  local copies, waits for them, and re-layouts  137 us (14%)
  matrix products  74.5 us (8%)
  other arithmetic  54.3 us (6%)
  between operations  17.7 us (2%)
    unnamed x1, blocking collectives  315 us
    psum x1, waiting for transfers between devices, body(): lax.psum((grad_qkv, grad_out, grad_router, grad_gain_attention, grad_gain...  78.7 us
    psum x1, waiting for transfers between devices, body(): residual = inputs + lax.psum(attn_part, 'tensor')  66.8 us
    psum x1, waiting for transfers between devices, body(): lax.psum(entered_part.astype(jnp.bfloat16), 'tensor').astype(jnp.float32)  46.5 us
    all_gather x1, waiting for transfers between devices, body(): lax.all_gather(buffer_back, 'tensor', axis=2, tiled=True)  32 us
    all_to_all x1, waiting for transfers between devices, body(): lax.all_to_all(grad_send, 'expert', split_axis=0, concat_axis=0, tiled=True)  26.4 us
    psum x1, waiting for transfers between devices, body(): lax.psum(grad_expert_in.astype(jnp.bfloat16), 'dp').astype(jnp.float32)  23.6 us
  transfers between devices with their start and end apart: 9, of which 8 were waited for; matrix products, arithmetic and copies ran while one was open for 13% of the time, Pallas kernels for 0%

profile of v1, /device:TPU:0, one launch (start us, length us, event | category | flops | bytes accessed | tf_op | source)
XLA Modules:
  0.0 952.6 jit_solution(8300503203625529814)
XLA Ops:
  11.9 2.7 fusion.86
  25.2 2.8 fusion.91
  29.1 66.8 %all-reduce.15.cloned.1.call-done = f32[591,768]{1,0:T(8,128)} async-done(((f32[591,768]{1,0:T(8,128)}), f32[591,768]{1,0:T(8,128)}) %all-reduce.15.cloned.1.call-update) | async-done | bytes 1815568 | tf_op jit(solution)/shard_map/psum | solution.py:74
  101.6 3.9 reshape.430
  105.5 9.8 %scatter_custom_fusion = bf16[1476,768]{1,0:T(8,128)(2,1)S(1)} fusion(s32[1182]{0:T(1024)S(1)} %get-tuple-element.23, bf16[1182,768]{1,0:T(8,128)(2,1)} %reshape.430, bf16[]{:T(256)} %constant.55.clone.1), kind=kCustom, calls=%fused_computation.98 | custom fusion | bytes 2267648 | tf_op jit(solution)/shard_map/scatter | solution.py:87
  117.3 4.6 all-to-all-start
  124.8 3.1 mul.276
  127.9 5.5 mul.277
  137.4 15.1 %gather_fusion.2 = f32[1182]{0:T(1024)S(1)} fusion(f32[591,4]{0,1:T(4,128)S(1)} %fusion.75, s32[1182]{0:T(1024)S(1)} %reshape.420), kind=kCustom, calls=%fused_computation.2 | custom fusion | bytes 18912 | tf_op jit(solution)/shard_map/jit(take_along_axis)/gather | solution.py:112
  152.4 14.2 %scatter_custom_fusion.1 = bf16[1476,768]{1,0:T(8,128)(2,1)S(1)} fusion(s32[1182]{0:T(1024)S(1)} %get-tuple-element.23, f32[1182,768]{1,0:T(8,128)} %mul.277, f32[1182]{0:T(1024)S(1)} %select_select_fusion.1, bf16[]{:T(256)} %constant.55.clone.1), kind=kCustom, calls=%fused_computation.60 | custom fusion | flops 1815552 | bytes 5906434 | tf_op jit(solution)/shard_map/scatter | solution.py:130
  168.6 6.4 all-to-all-done
  174.9 3.6 all-to-all-start.2
  178.8 4.0 fusion.48
  185.0 12.8 %convolution_bitcast_fusion = f32[4,1,369,768]{3,2,0,1:T(8,128)} fusion(bf16[1,768,768]{2,1,0:T(8,128)(2,1)S(1)} %copy-done, f32[4,369,768]{2,1,0:T(8,128)S(1)} %fusion.48), kind=kOutput, calls=%fused_computation.49 | convolution fusion | flops 1814842368 | bytes 10248192 | tf_op jit(solution)/shard_map/sjcf,jfd->sjcd/dot_general | solution.py:94
  197.8 6.6 copy.113
  204.4 26.4 %all-to-all-done.2 = bf16[4,369,768]{2,1,0:T(8,128)(2,1)S(1)} async-done(((bf16[4,369,768]{2,1,0:T(8,128)(2,1)}), bf16[4,369,768]{2,1,0:T(8,128)(2,1)S(1)}, u32[]{:S(2)}, u32[]{:S(2)}) %all-to-all-start.2) | async-done | bytes 2267168 | tf_op jit(solution)/shard_map/all_to_all | solution.py:133
  230.8 14.2 %fusion.6 = bf16[4,1,369,768]{3,2,0,1:T(8,128)(2,1)S(1)} fusion(f32[4,369,768]{2,1,0:T(8,128)} %copy-done.60, bf16[4,369,768]{2,1,0:T(8,128)(2,1)S(1)} %all-to-all-done.2, bf16[1,768,768]{2,1,0:T(8,128)(2,1)S(1)} %copy-done), kind=kOutput, calls=%fused_computation.14 | convolution fusion | flops 1822777344 | bytes 10248192 | tf_op jit(solution)/shard_map/sjcd,jfd->sjcf/dot_general | solution.py:135
  246.5 4.2 fusion.26
  250.6 6.7 copy.119
  257.3 314.8 %all-reduce.24 = (bf16[4,1,369,768]{2,0,1,3:T(4,128)(2,1)}, bf16[4,1,369,768]{2,0,1,3:T(4,128)(2,1)}) all-reduce(f32[4,1,369,768]{2,0,1,3:T(4,128)} %copy.113, f32[4,1,369,768]{2,0,1,3:T(4,128)} %copy.119), channel_id=2, replica_groups=mesh['dp'=2,'expert'=4,'tensor'=4] {'tensor'}, use_global_device_ids=true, to_apply=%region_10.11.clone | all-reduce | flops 2267136 | bytes 13602816
  573.5 15.9 %all_to_all.20 = bf16[4,369,192]{1,2,0:T(8,128)(2,1)S(1)} all-to-all(bf16[4,369,192]{1,2,0:T(8,128)(2,1)S(1)} %copy.114), channel_id=1, replica_groups=mesh['dp'=2,'expert'=4,'tensor'=4] {'expert'}, dimensions={0} | all-to-all | bytes 1133568 | tf_op jit(solution)/shard_map/all_to_all | solution.py:100
  592.1 17.0 %all_to_all.21 = bf16[4,369,192]{1,2,0:T(8,128)(2,1)S(1)} all-to-all(bf16[4,369,192]{1,2,0:T(8,128)(2,1)S(1)} %copy.120), channel_id=1, replica_groups=mesh['dp'=2,'expert'=4,'tensor'=4] {'expert'}, dimensions={0} | all-to-all | bytes 1133568 | tf_op jit(solution)/shard_map/all_to_all | solution.py:151
  612.5 4.7 fusion.38
  617.3 9.1 all-gather.3.cloned.1.call-done
  626.3 5.3 reshape.451
  631.6 2.8 copy.141
  634.5 32.0 %all-gather.5.cloned.1.call-done = bf16[4,369,768]{1,0,2:T(4,128)(2,1)} async-done(((bf16[4,369,192]{1,0,2:T(4,128)(2,1)}), bf16[4,369,768]{1,0,2:T(4,128)(2,1)}) %all-gather.5.cloned.1.call-update) | async-done | bytes 2267152 | tf_op jit(solution)/shard_map/all_gather | solution.py:158
  666.4 5.3 reshape.452
  671.7 4.2 copy.142
  676.0 4.9 gather_fusion
  680.8 7.7 gather_fusion.1
  688.5 5.2 reshape.403
  693.7 5.1 reshape.401
  698.8 11.2 %multiply_reduce_fusion = (f32[591,2]{1,0:T(8,128)S(1)}, f32[591,768]{1,0:T(8,128)}) fusion(f32[591,2,768]{2,1,0:T(2,128)} %reshape.401, f32[591,768]{1,0:T(8,128)S(1)} %copy-done.9, f32[591,2]{1,0:T(8,128)S(1)} %select_select_fusion), kind=kLoop, calls=%fused_computation.33 | loop fusion | flops 3176034 | bytes 7271664 | tf_op jit(solution)/shard_map/reduce_sum | solution.py:116
  711.6 6.6 multiply_reduce_fusion.1
  732.3 14.2 %fusion.41 = bf16[1,768,768]{2,1,0:T(8,128)(2,1)} fusion(bf16[4,369,768]{2,1,0:T(8,128)(2,1)} %copy-done.19, f32[4,369,768]{2,1,0:T(8,128)} %copy-done.60), kind=kOutput, calls=%fused_computation.77 | convolution fusion | flops 1815432192 | bytes 7981056 | tf_op jit(solution)/shard_map/sjcf,sjcd->jfd/dot_general | solution.py:138
  746.6 3.0 bitcast_convert_fusion.2
  749.7 78.7 %all-reduce.19.cloned.1.call-done = (f32[3,768,192]{1,2,0:T(8,128)}, f32[192,768]{1,0:T(8,128)}) async-done(((f32[3,768,192]{1,2,0:T(8,128)}, f32[192,768]{1,0:T(8,128)}), (f32[3,768,192]{1,2,0:T(8,128)}, f32[192,768]{1,0:T(8,128)})) %all-reduce.19.cloned.1.call-update) | async-done | bytes 2359312 | tf_op jit(solution)/shard_map/psum | solution.py:223
  828.5 23.6 %all-reduce.23.cloned.1.call-done = (bf16[1,768,768]{2,1,0:T(8,128)(2,1)}, bf16[1,768,768]{2,1,0:T(8,128)(2,1)}) async-done(((bf16[1,768,768]{2,1,0:T(8,128)(2,1)}, bf16[1,768,768]{2,1,0:T(8,128)(2,1)}), (bf16[1,768,768]{2,1,0:T(8,128)(2,1)}, bf16[1,768,768]{2,1,0:T(8,128)(2,1)})) %all-reduce.23.cloned.1.call-update) | async-done | bytes 2359312 | tf_op jit(solution)/shard_map/psum | solution.py:239
  852.1 2.8 convert_element_type.156
  854.9 2.9 convert_element_type.159
  857.8 2.3 reshape.392
  860.3 46.5 %all-reduce.17.cloned.1.call-done = bf16[591,768]{1,0:T(8,128)(2,1)} async-done(((bf16[591,768]{1,0:T(8,128)(2,1)}), bf16[591,768]{1,0:T(8,128)(2,1)}) %all-reduce.17.cloned.1.call-update) | async-done | bytes 907792 | tf_op jit(solution)/shard_map/psum | solution.py:214
  908.9 3.7 fusion.31
  912.6 2.9 reshape.399
  915.5 19.0 %all-reduce.3 = (f32[768,4]{0,1:T(4,128)S(1)}, f32[768]{0:T(1024)S(1)}, f32[768]{0:T(1024)S(1)}, f32[4]{0:T(128)S(1)}, f32[4]{0:T(128)S(1)}) all-reduce(f32[768,4]{0,1:T(4,128)S(1)} %fusion.92, f32[768]{0:T(1024)S(1)} %get-tuple-element.14, f32[768]{0:T(1024)S(1)} %copy-done.53, ...), channel_id=1, replica_groups=mesh['dp'=2,'expert'=4,'tensor'=4] {'expert'}, use_global_device_ids=true, to_apply=%region_28.29 | all-reduce | flops 4616 | bytes 36928 | tf_op jit(solution)/shard_map/psum | solution.py:223
  934.5 4.0 all-reduce.5
  939.8 2.8 copy.181
  (232 shorter events, 63.7 us)
Async XLA Ops:
  7.2 177.8 %copy-start = (bf16[1,768,768]{2,1,0:T(8,128)(2,1)S(1)}, bf16[1,768,768]{2,1,0:T(8,128)(2,1)}, u32[]{:S(2)}) copy-start(bf16[1,768,768]{2,1,0:T(8,128)(2,1)} %param.19) | copy-start | bytes 3538948
  7.2 4.7 copy-start.44
  7.2 88.7 %all-reduce.15.cloned.1.call-start = ((), (), s32[]{:S(2)}) async-start(), calls=%async_computation.4 | async-start | bytes 3637248 | tf_op jit(solution)/shard_map/psum | solution.py:74
  8.8 5.8 copy-start.35
  11.8 84.1 %copy-start.4 = (f32[591,768]{1,0:T(8,128)}, f32[591,768]{1,0:T(8,128)S(1)}, u32[]{:S(2)}) copy-start(f32[591,768]{1,0:T(8,128)S(1)} %reshape.400) | copy-start | bytes 5446660
  18.7 9.3 copy-start.15
  20.5 7.6 copy-start.41
  20.5 7.6 copy-start.52
  28.0 71.5 %copy-start.42 = (f32[768]{0:T(1024)S(1)}, f32[768]{0:T(1024)}, u32[]{:S(2)}) copy-start(f32[768]{0:T(1024)} %param.21) | copy-start | bytes 9220
  117.3 57.6 %all-to-all-start = ((bf16[4,369,768]{2,1,0:T(8,128)(2,1)}), bf16[4,369,768]{2,1,0:T(8,128)(2,1)}, u32[]{:S(2)}, u32[]{:S(2)}) async-start(bf16[4,369,768]{2,1,0:T(8,128)(2,1)} %reshape.386), calls=%async_computation | async-start | bytes 4620288 | tf_op jit(solution)/shard_map/all_to_all | solution.py:90
  124.8 8.6 copy-start.8
  127.9 5.5 copy-start.57
  127.9 6.7 copy-start.50
  174.9 55.9 %all-to-all-start.2 = ((bf16[4,369,768]{2,1,0:T(8,128)(2,1)}), bf16[4,369,768]{2,1,0:T(8,128)(2,1)S(1)}, u32[]{:S(2)}, u32[]{:S(2)}) async-start(bf16[4,369,768]{2,1,0:T(8,128)(2,1)} %reshape.394), calls=%async_computation.2 | async-start | bytes 4620288 | tf_op jit(solution)/shard_map/all_to_all | solution.py:133
  178.6 447.8 %all-gather.3.cloned.1.call-start = ((), (), s32[]{:S(2)}) async-start(), calls=%async_computation.5 | async-start | bytes 2949120 | tf_op jit(solution)/shard_map/all_gather | solution.py:107
  230.8 14.2 %copy-start.19 = (bf16[4,369,768]{2,1,0:T(8,128)(2,1)}, bf16[4,369,768]{2,1,0:T(8,128)(2,1)S(1)}, u32[]{:S(2)}) copy-start(bf16[4,369,768]{2,1,0:T(8,128)(2,1)S(1)} %all-to-all-done.2) | copy-start | bytes 6801412
  230.8 15.6 %copy-start.56 = (bf16[1,768,768]{2,1,0:T(8,128)(2,1)S(1)}, bf16[1,768,768]{2,1,0:T(8,128)(2,1)}, u32[]{:S(2)}) copy-start(bf16[1,768,768]{2,1,0:T(8,128)(2,1)} %param.18) | copy-start | bytes 3538948
  573.4 37.2 %copy-start.49 = (pred[3,197,2]{1,2,0:T(4,128)(4,1)S(1)}, pred[3,197,2]{1,2,0:T(4,128)(4,1)}, u32[]{:S(2)}) copy-start(pred[3,197,2]{1,2,0:T(4,128)(4,1)} %copy-done.48) | copy-start | bytes 3550
  573.4 37.2 %copy-start.32 = (s32[3,197,2]{1,0,2:T(4,128)S(1)}, s32[3,197,2]{1,0,2:T(4,128)}, u32[]{:S(2)}) copy-start(s32[3,197,2]{1,0,2:T(4,128)} %copy-done.31) | copy-start | bytes 14188
  573.5 38.6 %copy-start.47 = (s32[1182]{0:T(1024)S(1)}, s32[1182]{0:T(1024)}, u32[]{:S(2)}) copy-start(s32[1182]{0:T(1024)} %get-tuple-element.22) | copy-start | bytes 14188
  589.4 23.1 %copy-start.59 = (bf16[4,1,369,768]{3,2,0,1:T(8,128)(2,1)S(1)}, bf16[4,1,369,768]{3,2,0,1:T(8,128)(2,1)}, u32[]{:S(2)}) copy-start(bf16[4,1,369,768]{3,2,0,1:T(8,128)(2,1)} %copy-done.58) | copy-start | bytes 6801412
  590.7 75.8 %all-gather.5.cloned.1.call-start = ((), (), s32[]{:S(2)}) async-start(), calls=%async_computation.6 | async-start | bytes 2949120 | tf_op jit(solution)/shard_map/all_gather | solution.py:158
  610.3 218.1 %all-reduce.19.cloned.1.call-start = ((), (), s32[]{:S(2)}) async-start(), calls=%async_computation.8 | async-start | bytes 4718592 | tf_op jit(solution)/shard_map/psum | solution.py:223
  688.5 10.3 %copy-start.9 = (f32[591,768]{1,0:T(8,128)S(1)}, f32[591,768]{1,0:T(8,128)}, u32[]{:S(2)}) copy-start(f32[591,768]{1,0:T(8,128)} %copy-done.8) | copy-start | bytes 5446660
  698.8 12.0 %copy-start.26 = (f32[591,4]{0,1:T(4,128)S(1)}, f32[591,4]{0,1:T(4,128)}, u32[]{:S(2)}) copy-start(f32[591,4]{0,1:T(4,128)} %copy-done.25) | copy-start | bytes 28372
  698.8 12.0 %copy-start.28 = (f32[591]{0:T(1024)S(1)}, f32[591]{0:T(1024)}, u32[]{:S(2)}) copy-start(f32[591]{0:T(1024)} %copy-done.27) | copy-start | bytes 7096
  698.8 12.0 %copy-start.34 = (f32[591]{0:T(1024)S(1)}, f32[591]{0:T(1024)}, u32[]{:S(2)}) copy-start(f32[591]{0:T(1024)} %copy-done.33) | copy-start | bytes 7096
  698.8 12.7 %copy-start.21 = (f32[591,2]{1,0:T(8,128)S(1)}, f32[591,2]{1,0:T(8,128)}, u32[]{:S(2)}) copy-start(f32[591,2]{1,0:T(8,128)} %copy.123) | copy-start | bytes 14188
  710.0 8.2 copy-start.7
  710.0 8.2 copy-start.30
  710.0 8.2 copy-start.40
  710.0 8.3 copy-start.43
  710.0 8.3 copy-start.51
  711.6 8.3 copy-start.10
  711.6 8.3 copy-start.14
  725.9 4.0 copy-start.5
  725.9 4.0 copy-start.36
  725.9 4.0 copy-start.38
  726.0 4.0 copy-start.45
  732.3 119.8 %all-reduce.23.cloned.1.call-start = ((), (), s32[]{:S(2)}) async-start(), calls=%async_computation.10 | async-start | bytes 4718592 | tf_op jit(solution)/shard_map/psum | solution.py:239
  746.6 160.2 %all-reduce.17.cloned.1.call-start = ((), (), s32[]{:S(2)}) async-start(), calls=%async_computation.7 | async-start | bytes 1818624 | tf_op jit(solution)/shard_map/psum | solution.py:214
  749.7 190.1 %all-reduce.21.cloned.1.call-start = ((), (), s32[]{:S(2)}) async-start(), calls=%async_computation.9 | async-start | bytes 4718592 | tf_op jit(solution)/shard_map/psum | solution.py:222
  828.4 31.7 %copy-start.13 = (bf16[591,768]{1,0:T(8,128)(2,1)S(1)}, bf16[591,768]{1,0:T(8,128)(2,1)}, u32[]{:S(2)}) copy-start(bf16[591,768]{1,0:T(8,128)(2,1)} %copy-done.12) | copy-start | bytes 2723332
  854.9 53.9 %copy-start.46 = (f32[768]{0:T(1024)S(1)}, f32[768]{0:T(1024)}, u32[]{:S(2)}) copy-start(f32[768]{0:T(1024)} %param.20) | copy-start | bytes 9220
  908.9 6.6 copy-start.53
  908.9 6.6 copy-start.54
  908.9 6.6 copy-start.55
  908.9 35.6 %copy-start.1 = (bf16[1,768,768]{2,1,0:T(8,128)(2,1)S(1)}, bf16[1,768,768]{2,1,0:T(8,128)(2,1)}, u32[]{:S(2)}) copy-start(bf16[1,768,768]{2,1,0:T(8,128)(2,1)} %param.19) | copy-start | bytes 3538948
  (22 other events, 32.7 us)
Sparse Core Ops, SparseCore 0:
  28.1 67.6 all-reduce.14
  590.8 35.5 all-gather.2
  628.9 37.4 all-gather.4
  732.4 95.9 all-reduce.18
  831.3 20.7 all-reduce.22
  855.1 51.6 all-reduce.16
  909.3 21.7 all-reduce.20
